TPU v7x, 32 devices: a whole 2x2x4 slice. The times are simulated.
32 devices in a mesh: groups: 2 (over x), row: 16 (over z, y, core).
Axes of the slice: x: 2, y: 2, z: 4, core: 2. Of those that a mesh axis runs over, the one named last changes fastest.
Arguments:
- coupling: bfloat16 [32768, 896], P(('groups', 'row')), parts along dimension 0, may hold values from -6 to 6
- column_block: bfloat16 [32768, 1536], P(('groups', 'row')), parts along dimension 0, may hold values from -6 to 6
- pivot_inverse: bfloat16 [3072, 1536], P(('groups', 'row')), parts along dimension 0, may hold values from -0.15625 to 0.15625
- row_panel: bfloat16 [1536, 1792], P(None, ('groups', 'row')), parts along dimension 1, may hold values from -0.15625 to 0.15625
Outputs:
- lower_panel: bfloat16 [32768, 1536], P(('groups', 'row')), parts along dimension 0
- schur: bfloat16 [32768, 896], P(('groups', 'row')), parts along dimension 0
There are 2 independent parts, one for each index of `groups`. A program takes and returns all parts, laid end to end along the dimension named above; each array names one. Nothing has to cross between parts.
All inputs are finite; a program needn't handle non-finite values.
Results may differ from a plain program's by a relative error of at most 0.0039.
Values may be sent and summed in bfloat16 or wider, within the bound.
No kernel may reach another device: no remote copies, remote signals or barrier semaphores. Data moves between devices by JAX's collectives and lax.ppermute only.
A program may use at most 64 MiB of HBM per device.

v0:
```python
import jax
import jax.numpy as jnp
from jax import lax
from jax.sharding import PartitionSpec as P


def on_device(coupling, column_block, pivot_inverse, row_panel):
    whole_inverse = lax.all_gather(pivot_inverse, "row", axis=0, tiled=True)
    lower_panel = jnp.dot(column_block, whole_inverse, preferred_element_type=jnp.float32).astype(
        jnp.bfloat16
    )
    product = jnp.dot(
        lower_panel,
        lax.all_gather(row_panel, "row", axis=1, tiled=True),
        preferred_element_type=jnp.float32,
    )
    schur = (coupling.astype(jnp.float32) - product).astype(jnp.bfloat16)
    return (lower_panel, schur)


def solution(mesh):
    placed = (
        P(("groups", "row"), None),
        P(("groups", "row"), None),
        P(("groups", "row"), None),
        P(None, ("groups", "row")),
    )
    return jax.shard_map(
        on_device,
        mesh=mesh,
        in_specs=placed,
        out_specs=(P(("groups", "row"), None), P(("groups", "row"), None)),
        check_vma=False,
    )
```

profile of v0, /device:TPU:0, one launch (start us, length us, event | category | flops | bytes accessed | tf_op | source)
XLA Modules:
  0.0 125.8 jit_solution(16534755584395549889)
XLA Ops:
  7.2 0.0 copy-start
  7.2 0.0 all-gather.3.cloned.1.call-start
  7.2 0.7 all-gather.3.cloned.1.call-update
  7.9 0.0 all-gather.5.cloned.1.call-start
  8.0 0.7 all-gather.5.cloned.1.call-update
  8.7 57.8 %all-gather.3.cloned.1.call-done = bf16[1536,1536]{1,0:T(8,128)(2,1)} async-done(((bf16[96,1536]{1,0:T(8,128)(2,1)}), bf16[1536,1536]{1,0:T(8,128)(2,1)}) %all-gather.3.cloned.1.call-update) | async-done | bytes 4718608 | tf_op jit(solution)/shard_map/all_gather | solution.py:8
  66.4 0.0 copy-done
  66.4 8.7 %convolution_convert_fusion = bf16[1024,1536]{1,0:T(8,128)(2,1)} fusion(bf16[1024,1536]{1,0:T(8,128)(2,1)S(1)} %copy-done, bf16[1536,1536]{1,0:T(8,128)(2,1)} %all-gather.3.cloned.1.call-done), kind=kOutput, calls=%fused_computation | convolution fusion | flops 4833411072 | bytes 11010048 | tf_op jit(solution)/shard_map/dot_general | solution.py:9
  75.1 35.9 %all-gather.5.cloned.1.call-done = bf16[1536,896]{0,1:T(8,128)(2,1)} async-done(((bf16[1536,56]{0,1:T(8,128)(2,1)}), bf16[1536,896]{0,1:T(8,128)(2,1)}) %all-gather.5.cloned.1.call-update) | async-done | bytes 2752528 | tf_op jit(solution)/shard_map/all_gather | solution.py:14
  111.0 7.9 %subtract_convert_fusion = bf16[1024,896]{1,0:T(8,128)(2,1)} fusion(bf16[1024,896]{1,0:T(8,128)(2,1)} %param.4, bf16[1024,1536]{1,0:T(8,128)(2,1)} %convolution_convert_fusion, bf16[1536,896]{0,1:T(8,128)(2,1)} %all-gather.5.cloned.1.call-done), kind=kOutput, calls=%fused_computation.1 | convolution fusion | flops 2821324800 | bytes 9568256 | tf_op jit(solution)/shard_map/dot_general | solution.py:12
Async XLA Ops:
  7.2 59.3 %copy-start = (bf16[1024,1536]{1,0:T(8,128)(2,1)S(1)}, bf16[1024,1536]{1,0:T(8,128)(2,1)}, u32[]{:S(2)}) copy-start(bf16[1024,1536]{1,0:T(8,128)(2,1)} %param.5) | copy-start | bytes 9437188
  7.2 59.2 %all-gather.3.cloned.1.call-start = ((), (), s32[]{:S(2)}) async-start(), calls=%async_computation | async-start | bytes 5013504 | tf_op jit(solution)/shard_map/all_gather | solution.py:8
  7.9 103.1 %all-gather.5.cloned.1.call-start = ((), (), s32[]{:S(2)}) async-start(), calls=%async_computation.1 | async-start | bytes 2924544 | tf_op jit(solution)/shard_map/all_gather | solution.py:14
Sparse Core Ops, SparseCore 0:
  10.3 56.0 all-gather.2
  68.7 42.2 all-gather.4
where the time goes:
time: 126 us
  waiting for transfers between devices  95 us (75%)
  matrix products  16.6 us (13%)
  between operations  14 us (11%)
    all_gather x1, waiting for transfers between devices, on_device(): whole_inverse = lax.all_gather(pivot_inverse, 'row', axis=0, tiled=True)  57.8 us
    all_gather x1, waiting for transfers between devices, on_device(): lax.all_gather(row_panel, 'row', axis=1, tiled=True)  35.9 us
    dot_general x1, matrix products, on_device(): jnp.dot(column_block, whole_inverse, preferred_element_type=jnp.float32)  8.69 us
    dot_general x1, matrix products, on_device(): jnp.dot(lower_panel, lax.all_gather(row_panel, 'row', axis=1, tiled=True)...  7.92 us
  transfers between devices with their start and end apart: 2, of which 2 were waited for; matrix products, arithmetic and copies ran while one was open for 7% of the time, Pallas kernels for 0%

commit v1 on v0

--- a/solution.py
+++ b/solution.py
@@ -4,8 +4,20 @@
 from jax.sharding import PartitionSpec as P
 
 
+def ring_gather(array, axis, dim):
+    ways, here, step = (lax.axis_size(axis), lax.axis_index(axis), array.shape[dim])
+    dims = [n * ways if d == dim else n for d, n in enumerate(array.shape)]
+    full = lax.dynamic_update_slice_in_dim(
+        jnp.zeros(dims, array.dtype), array, here * step, axis=dim
+    )
+    for far in range(1, ways):
+        array = lax.ppermute(array, axis, [(d, (d + 1) % ways) for d in range(ways)])
+        full = lax.dynamic_update_slice_in_dim(full, array, (here - far) % ways * step, axis=dim)
+    return full
+
+
 def on_device(coupling, column_block, pivot_inverse, row_panel):
-    whole_inverse = lax.all_gather(pivot_inverse, "row", axis=0, tiled=True)
+    whole_inverse = ring_gather(pivot_inverse, "row", 0)
     lower_panel = jnp.dot(column_block, whole_inverse, preferred_element_type=jnp.float32).astype(
         jnp.bfloat16
     )

time: 126 us -> 176 us (1.40)
  waiting for transfers between devices: 95 us -> 135 us
  local copies, waits for them, and re-layouts: 0.01 us -> 11.1 us
  matrix products: 16.6 us -> 14.5 us
    ppermute x0 -> x15, waiting for transfers between devices: none -> 135 us  [ring_gather(): lax.ppermute(array, axis, [(d, (d + 1) % ways) for d in range(ways)])]
    all_gather x1 -> x0, waiting for transfers between devices: 57.8 us -> none  [on_device(): whole_inverse = lax.all_gather(pivot_inverse, 'row', axis=0, tiled=True)]
    all_gather x1, waiting for transfers between devices: 35.9 us -> 0.01 us  [on_device(): lax.all_gather(row_panel, 'row', axis=1, tiled=True)]
    unnamed x2 -> x25, local copies, waits for them, and re-layouts: 0.01 us -> 7.52 us
    dynamic_update_slice x0 -> x16, local copies, waits for them, and re-layouts: none -> 3.29 us  [the longest x15 3.26 us: ring_gather(): lax.dynamic_update_slice_in_dim(full, array, (here - far) % ways * step,...]
    dot_general x1, matrix products: 8.69 us -> 6.61 us  [on_device(): jnp.dot(column_block, whole_inverse, preferred_element_type=jnp.float32)]
  transfers between devices with their start and end apart: 2 -> 16, of which waited for: 2 -> 15; matrix products, arithmetic and copies ran while one was open for 7% -> 8% of each run, Pallas kernels for 0% -> 0%
where the time goes in v1:
time: 176 us
  waiting for transfers between devices  135 us (77%)
  matrix products  14.5 us (8%)
  between operations  14.2 us (8%)
  local copies, waits for them, and re-layouts  11.1 us (6%)
    ppermute x15, waiting for transfers between devices, ring_gather(): lax.ppermute(array, axis, [(d, (d + 1) % ways) for d in range(ways)])  135 us
    dot_general x1, matrix products, on_device(): jnp.dot(lower_panel, lax.all_gather(row_panel, 'row', axis=1, tiled=True)...  7.94 us
    unnamed x25, local copies, waits for them, and re-layouts  7.52 us
    dot_general x1, matrix products, on_device(): jnp.dot(column_block, whole_inverse, preferred_element_type=jnp.float32)  6.61 us
  transfers between devices with their start and end apart: 16, of which 15 were waited for; matrix products, arithmetic and copies ran while one was open for 8% of the time, Pallas kernels for 0%

profile of v1, /device:TPU:0, one launch (start us, length us, event | category | flops | bytes accessed | tf_op | source)
XLA Modules:
  0.0 175.8 jit_solution(11581055506412197121)
XLA Ops:
  7.2 0.0 copy-start
  7.2 0.0 copy-start.1
  7.2 0.0 all-gather.2.cloned.1.call-start
  7.2 0.5 collective-permute-start
  7.7 9.6 %collective-permute-done = bf16[96,1536]{1,0:T(8,128)(2,1)S(1)} collective-permute-done((bf16[96,1536]{1,0:T(8,128)(2,1)}, bf16[96,1536]{1,0:T(8,128)(2,1)S(1)}, u32[]{:S(2)}, u32[]{:S(2)}) %collective-permute-start) | collective-permute-done | bytes 294944 | tf_op jit(solution)/shard_map/ppermute | solution.py:14
  17.4 0.0 collective-permute-start.1
  17.4 0.7 copy-done.6
  18.1 8.1 %collective-permute-done.1 = bf16[96,1536]{1,0:T(8,128)(2,1)S(1)} collective-permute-done((bf16[96,1536]{1,0:T(8,128)(2,1)S(1)}, bf16[96,1536]{1,0:T(8,128)(2,1)S(1)}, u32[]{:S(2)}, u32[]{:S(2)}) %collective-permute-start.1) | collective-permute-done | bytes 294944 | tf_op jit(solution)/shard_map/ppermute | solution.py:14
  26.2 0.0 collective-permute-start.2
  26.2 0.7 copy-done.10
  26.9 8.1 %collective-permute-done.2 = bf16[96,1536]{1,0:T(8,128)(2,1)S(1)} collective-permute-done((bf16[96,1536]{1,0:T(8,128)(2,1)S(1)}, bf16[96,1536]{1,0:T(8,128)(2,1)S(1)}, u32[]{:S(2)}, u32[]{:S(2)}) %collective-permute-start.2) | collective-permute-done | bytes 294944 | tf_op jit(solution)/shard_map/ppermute | solution.py:14
  35.0 0.0 collective-permute-start.3
  35.1 0.7 copy-done.4
  35.8 8.1 %collective-permute-done.3 = bf16[96,1536]{1,0:T(8,128)(2,1)S(1)} collective-permute-done((bf16[96,1536]{1,0:T(8,128)(2,1)S(1)}, bf16[96,1536]{1,0:T(8,128)(2,1)S(1)}, u32[]{:S(2)}, u32[]{:S(2)}) %collective-permute-start.3) | collective-permute-done | bytes 294944 | tf_op jit(solution)/shard_map/ppermute | solution.py:14
  43.9 0.0 collective-permute-start.4
  43.9 8.8 %collective-permute-done.4 = bf16[96,1536]{1,0:T(8,128)(2,1)S(1)} collective-permute-done((bf16[96,1536]{1,0:T(8,128)(2,1)S(1)}, bf16[96,1536]{1,0:T(8,128)(2,1)S(1)}, u32[]{:S(2)}, u32[]{:S(2)}) %collective-permute-start.4) | collective-permute-done | bytes 294944 | tf_op jit(solution)/shard_map/ppermute | solution.py:14
  52.7 0.7 copy-done.2
  53.5 0.0 collective-permute-start.5
  53.5 8.9 %collective-permute-done.5 = bf16[96,1536]{1,0:T(8,128)(2,1)} collective-permute-done((bf16[96,1536]{1,0:T(8,128)(2,1)S(1)}, bf16[96,1536]{1,0:T(8,128)(2,1)}, u32[]{:S(2)}, u32[]{:S(2)}) %collective-permute-start.5) | collective-permute-done | bytes 294944 | tf_op jit(solution)/shard_map/ppermute | solution.py:14
  62.4 0.0 collective-permute-start.6
  62.4 0.0 all-gather.2.cloned.1.call-update
  62.4 9.1 %collective-permute-done.6 = bf16[96,1536]{1,0:T(8,128)(2,1)} collective-permute-done((bf16[96,1536]{1,0:T(8,128)(2,1)}, bf16[96,1536]{1,0:T(8,128)(2,1)}, u32[]{:S(2)}, u32[]{:S(2)}) %collective-permute-start.6) | collective-permute-done | bytes 294944 | tf_op jit(solution)/shard_map/ppermute | solution.py:14
  71.6 0.0 collective-permute-start.7
  71.6 0.0 copy-start.9
  71.6 0.0 copy-start.3
  71.6 0.3 broadcast_in_dim.3
  72.0 13.0 %collective-permute-done.7 = bf16[96,1536]{1,0:T(8,128)(2,1)} collective-permute-done((bf16[96,1536]{1,0:T(8,128)(2,1)}, bf16[96,1536]{1,0:T(8,128)(2,1)}, u32[]{:S(2)}, u32[]{:S(2)}) %collective-permute-start.7) | collective-permute-done | bytes 294944 | tf_op jit(solution)/shard_map/ppermute | solution.py:14
  84.9 0.0 collective-permute-start.8
  85.0 9.1 %collective-permute-done.8 = bf16[96,1536]{1,0:T(8,128)(2,1)S(1)} collective-permute-done((bf16[96,1536]{1,0:T(8,128)(2,1)}, bf16[96,1536]{1,0:T(8,128)(2,1)S(1)}, u32[]{:S(2)}, u32[]{:S(2)}) %collective-permute-start.8) | collective-permute-done | bytes 294944 | tf_op jit(solution)/shard_map/ppermute | solution.py:14
  94.1 0.0 collective-permute-start.9
  94.1 0.0 copy-done.5
  94.2 11.3 %collective-permute-done.9 = bf16[96,1536]{1,0:T(8,128)(2,1)S(1)} collective-permute-done((bf16[96,1536]{1,0:T(8,128)(2,1)S(1)}, bf16[96,1536]{1,0:T(8,128)(2,1)S(1)}, u32[]{:S(2)}, u32[]{:S(2)}) %collective-permute-start.9) | collective-permute-done | bytes 294944 | tf_op jit(solution)/shard_map/ppermute | solution.py:14
  105.5 0.0 collective-permute-start.10
  105.5 1.0 constant_dynamic-update-slice_fusion.9
  106.5 7.8 %collective-permute-done.10 = bf16[96,1536]{1,0:T(8,128)(2,1)S(1)} collective-permute-done((bf16[96,1536]{1,0:T(8,128)(2,1)S(1)}, bf16[96,1536]{1,0:T(8,128)(2,1)S(1)}, u32[]{:S(2)}, u32[]{:S(2)}) %collective-permute-start.10) | collective-permute-done | bytes 294944 | tf_op jit(solution)/shard_map/ppermute | solution.py:14
  114.3 0.0 collective-permute-start.11
  114.3 1.0 constant_dynamic-update-slice_fusion.8
  115.3 1.0 constant_dynamic-update-slice_fusion.7
  116.3 6.9 %collective-permute-done.11 = bf16[96,1536]{1,0:T(8,128)(2,1)S(1)} collective-permute-done((bf16[96,1536]{1,0:T(8,128)(2,1)S(1)}, bf16[96,1536]{1,0:T(8,128)(2,1)S(1)}, u32[]{:S(2)}, u32[]{:S(2)}) %collective-permute-start.11) | collective-permute-done | bytes 294944 | tf_op jit(solution)/shard_map/ppermute | solution.py:14
  123.2 0.0 collective-permute-start.12
  123.3 8.8 %collective-permute-done.12 = bf16[96,1536]{1,0:T(8,128)(2,1)S(1)} collective-permute-done((bf16[96,1536]{1,0:T(8,128)(2,1)S(1)}, bf16[96,1536]{1,0:T(8,128)(2,1)S(1)}, u32[]{:S(2)}, u32[]{:S(2)}) %collective-permute-start.12) | collective-permute-done | bytes 294944 | tf_op jit(solution)/shard_map/ppermute | solution.py:14
  132.0 0.0 collective-permute-start.13
  132.1 8.8 %collective-permute-done.13 = bf16[96,1536]{1,0:T(8,128)(2,1)S(1)} collective-permute-done((bf16[96,1536]{1,0:T(8,128)(2,1)S(1)}, bf16[96,1536]{1,0:T(8,128)(2,1)S(1)}, u32[]{:S(2)}, u32[]{:S(2)}) %collective-permute-start.13) | collective-permute-done | bytes 294944 | tf_op jit(solution)/shard_map/ppermute | solution.py:14
  140.9 0.0 collective-permute-start.14
  140.9 8.8 %collective-permute-done.14 = bf16[96,1536]{1,0:T(8,128)(2,1)S(1)} collective-permute-done((bf16[96,1536]{1,0:T(8,128)(2,1)S(1)}, bf16[96,1536]{1,0:T(8,128)(2,1)S(1)}, u32[]{:S(2)}, u32[]{:S(2)}) %collective-permute-start.14) | collective-permute-done | bytes 294944 | tf_op jit(solution)/shard_map/ppermute | solution.py:14
  149.8 6.6 %convolution_convert_fusion = bf16[1536,1024]{1,0:T(8,128)(2,1)} fusion(bf16[1536,1536]{1,0:T(8,128)(2,1)S(1)} %constant_dynamic-update-slice_fusion, bf16[1024,1536]{1,0:T(8,128)(2,1)S(1)} %copy-done), kind=kOutput, calls=%fused_computation | convolution fusion | flops 4833411072 | bytes 11010048 | tf_op jit(solution)/shard_map/dot_general | solution.py:21
  156.4 4.6 %copy.6 = bf16[1024,1536]{1,0:T(8,128)(2,1)} copy(bf16[1024,1536]{0,1:T(8,128)(2,1)} %bitcast.5) | data formatting | bytes 6291456
  161.0 7.9 %subtract_convert_fusion = bf16[1024,896]{1,0:T(8,128)(2,1)} fusion(bf16[1024,896]{1,0:T(8,128)(2,1)} %param.4, bf16[1536,1024]{1,0:T(8,128)(2,1)} %convolution_convert_fusion, bf16[1536,896]{0,1:T(8,128)(2,1)} %all-gather.2.cloned.1.call-done), kind=kOutput, calls=%fused_computation.1 | convolution fusion | flops 2821324800 | bytes 9568256 | tf_op jit(solution)/shard_map/dot_general | solution.py:24
  (29 shorter events, 0.4 us)
Async XLA Ops:
  7.2 142.6 %copy-start = (bf16[1024,1536]{1,0:T(8,128)(2,1)S(1)}, bf16[1024,1536]{1,0:T(8,128)(2,1)}, u32[]{:S(2)}) copy-start(bf16[1024,1536]{1,0:T(8,128)(2,1)} %param.5) | copy-start | bytes 9437188
  7.2 64.7 %copy-start.1 = (bf16[96,1536]{1,0:T(8,128)(2,1)S(1)}, bf16[96,1536]{1,0:T(8,128)(2,1)}, u32[]{:S(2)}) copy-start(bf16[96,1536]{1,0:T(8,128)(2,1)} %param.6) | copy-start | bytes 884740
  7.2 153.8 %all-gather.2.cloned.1.call-start = ((), (), s32[]{:S(2)}) async-start(), calls=%async_computation | async-start | bytes 2924544 | tf_op jit(solution)/shard_map/all_gather | solution.py:26
  7.2 10.1 %collective-permute-start = (bf16[96,1536]{1,0:T(8,128)(2,1)}, bf16[96,1536]{1,0:T(8,128)(2,1)S(1)}, u32[]{:S(2)}, u32[]{:S(2)}) collective-permute-start(bf16[96,1536]{1,0:T(8,128)(2,1)} %param.6), channel_id=1, source_target_pairs={{0,1},{1,2},{2,3},{3,4},{4,5},{5,6},{6,7},{7,8},{8,9},{9,10},{10,1... | collective-permute-start | bytes 884744 | tf_op jit(solution)/shard_map/ppermute | solution.py:14
  17.4 0.7 copy-start.6
  17.4 8.8 %collective-permute-start.1 = (bf16[96,1536]{1,0:T(8,128)(2,1)S(1)}, bf16[96,1536]{1,0:T(8,128)(2,1)S(1)}, u32[]{:S(2)}, u32[]{:S(2)}) collective-permute-start(bf16[96,1536]{1,0:T(8,128)(2,1)S(1)} %collective-permute-done), channel_id=1, source_target_pairs={{0,1},{1,2},{2,3},{3,4},{4,5},{5,6},{6,7},{7,8},{8,9},{9,10},{10,1... | collective-permute-start | bytes 884744 | tf_op jit(solution)/shard_map/ppermute | solution.py:14
  26.2 0.7 copy-start.10
  26.2 8.8 %collective-permute-start.2 = (bf16[96,1536]{1,0:T(8,128)(2,1)S(1)}, bf16[96,1536]{1,0:T(8,128)(2,1)S(1)}, u32[]{:S(2)}, u32[]{:S(2)}) collective-permute-start(bf16[96,1536]{1,0:T(8,128)(2,1)S(1)} %collective-permute-done.1), channel_id=1, source_target_pairs={{0,1},{1,2},{2,3},{3,4},{4,5},{5,6},{6,7},{7,8},{8,9},{9,10},{10,1... | collective-permute-start | bytes 884744 | tf_op jit(solution)/shard_map/ppermute | solution.py:14
  35.0 0.7 copy-start.4
  35.0 8.8 %collective-permute-start.3 = (bf16[96,1536]{1,0:T(8,128)(2,1)S(1)}, bf16[96,1536]{1,0:T(8,128)(2,1)S(1)}, u32[]{:S(2)}, u32[]{:S(2)}) collective-permute-start(bf16[96,1536]{1,0:T(8,128)(2,1)S(1)} %collective-permute-done.2), channel_id=1, source_target_pairs={{0,1},{1,2},{2,3},{3,4},{4,5},{5,6},{6,7},{7,8},{8,9},{9,10},{10,1... | collective-permute-start | bytes 884744 | tf_op jit(solution)/shard_map/ppermute | solution.py:14
  43.9 18.5 %copy-start.8 = (bf16[96,1536]{1,0:T(8,128)(2,1)}, bf16[96,1536]{1,0:T(8,128)(2,1)S(1)}, u32[]{:S(2)}) copy-start(bf16[96,1536]{1,0:T(8,128)(2,1)S(1)} %collective-permute-done.3) | copy-start | bytes 884740
  43.9 8.8 %collective-permute-start.4 = (bf16[96,1536]{1,0:T(8,128)(2,1)S(1)}, bf16[96,1536]{1,0:T(8,128)(2,1)S(1)}, u32[]{:S(2)}, u32[]{:S(2)}) collective-permute-start(bf16[96,1536]{1,0:T(8,128)(2,1)S(1)} %collective-permute-done.3), channel_id=1, source_target_pairs={{0,1},{1,2},{2,3},{3,4},{4,5},{5,6},{6,7},{7,8},{8,9},{9,10},{10,1... | collective-permute-start | bytes 884744 | tf_op jit(solution)/shard_map/ppermute | solution.py:14
  52.7 0.7 copy-start.2
  53.5 9.0 %collective-permute-start.5 = (bf16[96,1536]{1,0:T(8,128)(2,1)S(1)}, bf16[96,1536]{1,0:T(8,128)(2,1)}, u32[]{:S(2)}, u32[]{:S(2)}) collective-permute-start(bf16[96,1536]{1,0:T(8,128)(2,1)S(1)} %collective-permute-done.4), channel_id=1, source_target_pairs={{0,1},{1,2},{2,3},{3,4},{4,5},{5,6},{6,7},{7,8},{8,9},{9,10},{10,1... | collective-permute-start | bytes 884744 | tf_op jit(solution)/shard_map/ppermute | solution.py:14
  62.4 9.2 %collective-permute-start.6 = (bf16[96,1536]{1,0:T(8,128)(2,1)}, bf16[96,1536]{1,0:T(8,128)(2,1)}, u32[]{:S(2)}, u32[]{:S(2)}) collective-permute-start(bf16[96,1536]{1,0:T(8,128)(2,1)} %collective-permute-done.5), channel_id=1, source_target_pairs={{0,1},{1,2},{2,3},{3,4},{4,5},{5,6},{6,7},{7,8},{8,9},{9,10},{10,1... | collective-permute-start | bytes 884744 | tf_op jit(solution)/shard_map/ppermute | solution.py:14
  71.6 13.4 %collective-permute-start.7 = (bf16[96,1536]{1,0:T(8,128)(2,1)}, bf16[96,1536]{1,0:T(8,128)(2,1)}, u32[]{:S(2)}, u32[]{:S(2)}) collective-permute-start(bf16[96,1536]{1,0:T(8,128)(2,1)} %collective-permute-done.6), channel_id=1, source_target_pairs={{0,1},{1,2},{2,3},{3,4},{4,5},{5,6},{6,7},{7,8},{8,9},{9,10},{10,1... | collective-permute-start | bytes 884744 | tf_op jit(solution)/shard_map/ppermute | solution.py:14
  71.6 13.4 %copy-start.7 = (bf16[96,1536]{1,0:T(8,128)(2,1)S(1)}, bf16[96,1536]{1,0:T(8,128)(2,1)}, u32[]{:S(2)}) copy-start(bf16[96,1536]{1,0:T(8,128)(2,1)} %copy-done.6) | copy-start | bytes 884740
  71.6 13.4 %copy-start.11 = (bf16[96,1536]{1,0:T(8,128)(2,1)S(1)}, bf16[96,1536]{1,0:T(8,128)(2,1)}, u32[]{:S(2)}) copy-start(bf16[96,1536]{1,0:T(8,128)(2,1)} %copy-done.10) | copy-start | bytes 884740
  71.6 22.5 %copy-start.5 = (bf16[96,1536]{1,0:T(8,128)(2,1)S(1)}, bf16[96,1536]{1,0:T(8,128)(2,1)}, u32[]{:S(2)}) copy-start(bf16[96,1536]{1,0:T(8,128)(2,1)} %copy-done.4) | copy-start | bytes 884740
  71.6 22.5 %copy-start.9 = (bf16[96,1536]{1,0:T(8,128)(2,1)S(1)}, bf16[96,1536]{1,0:T(8,128)(2,1)}, u32[]{:S(2)}) copy-start(bf16[96,1536]{1,0:T(8,128)(2,1)} %copy-done.8) | copy-start | bytes 884740
  71.6 33.9 %copy-start.3 = (bf16[96,1536]{1,0:T(8,128)(2,1)S(1)}, bf16[96,1536]{1,0:T(8,128)(2,1)}, u32[]{:S(2)}) copy-start(bf16[96,1536]{1,0:T(8,128)(2,1)} %copy-done.2) | copy-start | bytes 884740
  84.9 9.2 %collective-permute-start.8 = (bf16[96,1536]{1,0:T(8,128)(2,1)}, bf16[96,1536]{1,0:T(8,128)(2,1)S(1)}, u32[]{:S(2)}, u32[]{:S(2)}) collective-permute-start(bf16[96,1536]{1,0:T(8,128)(2,1)} %collective-permute-done.7), channel_id=1, source_target_pairs={{0,1},{1,2},{2,3},{3,4},{4,5},{5,6},{6,7},{7,8},{8,9},{9,10},{10,1... | collective-permute-start | bytes 884744 | tf_op jit(solution)/shard_map/ppermute | solution.py:14
  94.1 11.4 %collective-permute-start.9 = (bf16[96,1536]{1,0:T(8,128)(2,1)S(1)}, bf16[96,1536]{1,0:T(8,128)(2,1)S(1)}, u32[]{:S(2)}, u32[]{:S(2)}) collective-permute-start(bf16[96,1536]{1,0:T(8,128)(2,1)S(1)} %collective-permute-done.8), channel_id=1, source_target_pairs={{0,1},{1,2},{2,3},{3,4},{4,5},{5,6},{6,7},{7,8},{8,9},{9,10},{10,1... | collective-permute-start | bytes 884744 | tf_op jit(solution)/shard_map/ppermute | solution.py:14
  105.5 8.8 %collective-permute-start.10 = (bf16[96,1536]{1,0:T(8,128)(2,1)S(1)}, bf16[96,1536]{1,0:T(8,128)(2,1)S(1)}, u32[]{:S(2)}, u32[]{:S(2)}) collective-permute-start(bf16[96,1536]{1,0:T(8,128)(2,1)S(1)} %collective-permute-done.9), channel_id=1, source_target_pairs={{0,1},{1,2},{2,3},{3,4},{4,5},{5,6},{6,7},{7,8},{8,9},{9,10},{10,1... | collective-permute-start | bytes 884744 | tf_op jit(solution)/shard_map/ppermute | solution.py:14
  114.3 8.8 %collective-permute-start.11 = (bf16[96,1536]{1,0:T(8,128)(2,1)S(1)}, bf16[96,1536]{1,0:T(8,128)(2,1)S(1)}, u32[]{:S(2)}, u32[]{:S(2)}) collective-permute-start(bf16[96,1536]{1,0:T(8,128)(2,1)S(1)} %collective-permute-done.10), channel_id=1, source_target_pairs={{0,1},{1,2},{2,3},{3,4},{4,5},{5,6},{6,7},{7,8},{8,9},{9,10},{10,1... | collective-permute-start | bytes 884744 | tf_op jit(solution)/shard_map/ppermute | solution.py:14
  123.2 8.8 %collective-permute-start.12 = (bf16[96,1536]{1,0:T(8,128)(2,1)S(1)}, bf16[96,1536]{1,0:T(8,128)(2,1)S(1)}, u32[]{:S(2)}, u32[]{:S(2)}) collective-permute-start(bf16[96,1536]{1,0:T(8,128)(2,1)S(1)} %collective-permute-done.11), channel_id=1, source_target_pairs={{0,1},{1,2},{2,3},{3,4},{4,5},{5,6},{6,7},{7,8},{8,9},{9,10},{10,1... | collective-permute-start | bytes 884744 | tf_op jit(solution)/shard_map/ppermute | solution.py:14
  132.0 8.8 %collective-permute-start.13 = (bf16[96,1536]{1,0:T(8,128)(2,1)S(1)}, bf16[96,1536]{1,0:T(8,128)(2,1)S(1)}, u32[]{:S(2)}, u32[]{:S(2)}) collective-permute-start(bf16[96,1536]{1,0:T(8,128)(2,1)S(1)} %collective-permute-done.12), channel_id=1, source_target_pairs={{0,1},{1,2},{2,3},{3,4},{4,5},{5,6},{6,7},{7,8},{8,9},{9,10},{10,1... | collective-permute-start | bytes 884744 | tf_op jit(solution)/shard_map/ppermute | solution.py:14
  140.9 8.8 %collective-permute-start.14 = (bf16[96,1536]{1,0:T(8,128)(2,1)S(1)}, bf16[96,1536]{1,0:T(8,128)(2,1)S(1)}, u32[]{:S(2)}, u32[]{:S(2)}) collective-permute-start(bf16[96,1536]{1,0:T(8,128)(2,1)S(1)} %collective-permute-done.13), channel_id=1, source_target_pairs={{0,1},{1,2},{2,3},{3,4},{4,5},{5,6},{6,7},{7,8},{8,9},{9,10},{10,1... | collective-permute-start | bytes 884744 | tf_op jit(solution)/shard_map/ppermute | solution.py:14
Sparse Core Ops, SparseCore 0:
  62.6 48.2 all-gather.1
